TPU v7x, 256 devices: a whole 4x4x8 slice. The times are simulated.
256 devices in a mesh: col: 64 (over z, x, core), rhs: 4 (over y).
Axes of the slice: x: 4, y: 4, z: 8, core: 2. Of those that a mesh axis runs over, the one named last changes fastest.
Arguments:
- rhs_block: bfloat16 [16384, 4096], P('col', 'rhs'), may hold values from -6 to 6
- solution: bfloat16 [196608, 4096], P('col', 'rhs'), may hold values from -6 to 6
- factor: bfloat16 [64, 6, 256, 3072], P('col', None, 'rhs'), may hold values from -0.109375 to 0.109375
- tile_list: int32 [64, 6], P('col'), may hold values 0 or 1
- diag_inverse: bfloat16 [64, 256, 256], P('col'), may hold values from -0.375 to 0.375
Outputs:
- solved_rows: bfloat16 [16384, 4096], P('col', 'rhs')
All inputs are finite; a program needn't handle non-finite values. No bound on the sum of `tile_list` on one device may be relied on, other than what follows from the above.
Results may differ from a plain program's by a relative error of at most 0.0049.
Values may be sent and summed in bfloat16 or wider, within the bound.
A program may use at most 64 MiB of HBM per device.

v0:
```python
import jax
import jax.numpy as jnp
from jax import lax
from jax.sharding import PartitionSpec as P


def from_behind(block, axis, distance):
    devices = range(lax.axis_size(axis))
    route = [((i - distance) % len(devices), i) for i in devices]
    return lax.ppermute(block, axis, route)


def per_device(rhs_block, solution, factor, tile_list, diag_inverse):
    hop_count = factor.shape[1]
    carried = jnp.zeros((rhs_block.shape[0], rhs_block.shape[1]), jnp.float32)
    for offset in reversed(range(hop_count)):
        product_term = jnp.dot(
            lax.all_gather(factor[0, offset], "rhs", axis=0, tiled=True),
            solution,
            preferred_element_type=jnp.float32,
        )
        carried = carried + product_term * tile_list[0, offset].astype(jnp.float32)
        carried = from_behind(carried, "col", 1)
    remaining = (rhs_block.astype(jnp.float32) - carried).astype(jnp.bfloat16)
    return jnp.dot(diag_inverse[0], remaining, preferred_element_type=jnp.float32).astype(
        jnp.bfloat16
    )


def solution(mesh):
    in_specs = (
        P("col", "rhs"),
        P("col", "rhs"),
        P("col", None, "rhs", None),
        P("col", None),
        P("col", None, None),
    )
    out_specs = P("col", "rhs")
    return jax.shard_map(
        per_device, mesh=mesh, in_specs=in_specs, out_specs=out_specs, check_vma=False
    )
```

profile of v0, /device:TPU:8, one launch (start us, length us, event | category | flops | bytes accessed | tf_op | source)
XLA Modules:
  0.0 225.7 jit_solution(13746546917414927949)
XLA Ops:
  6.5 3.0 %fusion.35 = (bf16[1,1,64,3072]{3,2,1,0:T(8,128)(2,1)}, bf16[1,1,64,3072]{3,2,1,0:T(8,128)(2,1)}, bf16[1,1,64,3072]{3,2,1,0:T(8,128)(2,1)}, bf16[1,1,64,3072]{3,...) fusion(bf16[1,6,64,3072]{3,2,1,0:T(8,128)(2,1)} %param.7), kind=kLoop, calls=%fused_computation.23 | loop fusion | bytes 4718592 | tf_op jit(solution)/shard_map/slice | solution.py:18
  9.6 0.0 all-gather.15.cloned.1.call-start
  9.7 0.7 all-gather.15.cloned.1.call-update
  10.4 0.7 all-gather.17.cloned.1.call-update
  11.1 0.5 all-gather.19.cloned.1.call-update
  11.7 0.7 fusion.36
  13.0 27.7 %all-gather.13.cloned.1.call-done = bf16[1,1,256,3072]{3,2,1,0:T(8,128)(2,1)} async-done(((bf16[1,1,64,3072]{3,2,1,0:T(8,128)(2,1)}), bf16[1,1,256,3072]{3,2,1,0:T(8,128)(2,1)}) %all-gather.13.cloned.1.call-update) | async-done | bytes 1572880 | tf_op jit(solution)/shard_map/all_gather | solution.py:18
  40.7 5.1 %fusion.12 = f32[256,1024]{1,0:T(8,128)S(1)} fusion(bf16[3072,1024]{1,0:T(8,128)(2,1)} %param.6, bf16[1,1,256,3072]{3,2,1,0:T(8,128)(2,1)} %all-gather.13.cloned.1.call-done, f32[]{:T(128)} %bitcast.1), kind=kOutput, calls=%fused_computation.12 | convolution fusion | flops 1610874880 | bytes 8912900 | tf_op jit(solution)/shard_map/dot_general | solution.py:17
  45.8 0.1 collective-permute-start
  45.9 0.0 all-gather.23.cloned.1.call-start
  46.5 25.1 %all-gather.15.cloned.1.call-done = bf16[1,1,256,3072]{3,2,1,0:T(8,128)(2,1)} async-done(((bf16[1,1,64,3072]{3,2,1,0:T(8,128)(2,1)}), bf16[1,1,256,3072]{3,2,1,0:T(8,128)(2,1)}) %all-gather.15.cloned.1.call-update) | async-done | bytes 1572880 | tf_op jit(solution)/shard_map/all_gather | solution.py:18
  71.5 5.1 %fusion.30 = f32[256,1024]{1,0:T(8,128)S(1)} fusion(f32[256,1024]{1,0:T(8,128)S(1)} %collective-permute-done, bf16[3072,1024]{1,0:T(8,128)(2,1)} %param.6, bf16[1,1,256,3072]{3,2,1,0:T(8,128)(2,1)} %all-gather.15.cloned.1.call-done, f32[]{:T(128)} %bitcast.3), kind=kOutput, calls=%fused_computation.18 | convolution fusion | flops 1611137024 | bytes 9961476 | tf_op jit(solution)/shard_map/dot_general | solution.py:17
  76.6 0.1 collective-permute-start.1
  77.3 25.1 %all-gather.17.cloned.1.call-done = bf16[1,1,256,3072]{3,2,1,0:T(8,128)(2,1)} async-done(((bf16[1,1,64,3072]{3,2,1,0:T(8,128)(2,1)}), bf16[1,1,256,3072]{3,2,1,0:T(8,128)(2,1)}) %all-gather.17.cloned.1.call-update) | async-done | bytes 1572880 | tf_op jit(solution)/shard_map/all_gather | solution.py:18
  102.4 5.1 %fusion.18 = f32[256,1024]{1,0:T(8,128)S(1)} fusion(bf16[3072,1024]{1,0:T(8,128)(2,1)} %param.6, bf16[1,1,256,3072]{3,2,1,0:T(8,128)(2,1)} %all-gather.17.cloned.1.call-done, f32[]{:T(128)} %bitcast.5), kind=kOutput, calls=%fused_computation.14 | convolution fusion | flops 1610874880 | bytes 8912900 | tf_op jit(solution)/shard_map/dot_general | solution.py:17
  107.5 0.2 add.16
  107.6 0.1 collective-permute-start.2
  108.3 24.8 %all-gather.19.cloned.1.call-done = bf16[1,1,256,3072]{3,2,1,0:T(8,128)(2,1)} async-done(((bf16[1,1,64,3072]{3,2,1,0:T(8,128)(2,1)}), bf16[1,1,256,3072]{3,2,1,0:T(8,128)(2,1)}) %all-gather.19.cloned.1.call-update) | async-done | bytes 1572880 | tf_op jit(solution)/shard_map/all_gather | solution.py:18
  133.1 5.1 %fusion.21 = f32[256,1024]{1,0:T(8,128)S(1)} fusion(bf16[3072,1024]{1,0:T(8,128)(2,1)} %param.6, bf16[1,1,256,3072]{3,2,1,0:T(8,128)(2,1)} %all-gather.19.cloned.1.call-done, f32[]{:T(128)} %bitcast.7), kind=kOutput, calls=%fused_computation.15 | convolution fusion | flops 1610874880 | bytes 8912900 | tf_op jit(solution)/shard_map/dot_general | solution.py:17
  138.2 0.2 add.17
  138.4 0.1 collective-permute-start.3
  139.1 24.7 %all-gather.21.cloned.1.call-done = bf16[1,1,256,3072]{3,2,1,0:T(8,128)(2,1)} async-done(((bf16[1,1,64,3072]{3,2,1,0:T(8,128)(2,1)}), bf16[1,1,256,3072]{3,2,1,0:T(8,128)(2,1)}) %all-gather.21.cloned.1.call-update) | async-done | bytes 1572880 | tf_op jit(solution)/shard_map/all_gather | solution.py:18
  163.8 5.1 %fusion.24 = f32[256,1024]{1,0:T(8,128)S(1)} fusion(bf16[3072,1024]{1,0:T(8,128)(2,1)} %param.6, bf16[1,1,256,3072]{3,2,1,0:T(8,128)(2,1)} %all-gather.21.cloned.1.call-done, f32[]{:T(128)} %bitcast.9), kind=kOutput, calls=%fused_computation.16 | convolution fusion | flops 1610874880 | bytes 8912900 | tf_op jit(solution)/shard_map/dot_general | solution.py:17
  168.9 0.2 add.18
  169.1 0.3 collective-permute-start.4
  170.0 24.6 %all-gather.23.cloned.1.call-done = bf16[1,1,256,3072]{3,2,1,0:T(8,128)(2,1)} async-done(((bf16[1,1,64,3072]{3,2,1,0:T(8,128)(2,1)}), bf16[1,1,256,3072]{3,2,1,0:T(8,128)(2,1)}) %all-gather.23.cloned.1.call-update) | async-done | bytes 1572880 | tf_op jit(solution)/shard_map/all_gather | solution.py:18
  194.5 5.1 %fusion.27 = f32[256,1024]{1,0:T(8,128)S(1)} fusion(bf16[3072,1024]{1,0:T(8,128)(2,1)} %param.6, bf16[1,1,256,3072]{3,2,1,0:T(8,128)(2,1)} %all-gather.23.cloned.1.call-done, f32[]{:T(128)} %bitcast.11), kind=kOutput, calls=%fused_computation.17 | convolution fusion | flops 1610874880 | bytes 8912900 | tf_op jit(solution)/shard_map/dot_general | solution.py:17
  199.6 0.2 add.19
  199.8 0.1 collective-permute-start.5
  199.9 17.5 %collective-permute-done.5 = f32[256,1024]{1,0:T(8,128)S(1)} collective-permute-done((f32[256,1024]{1,0:T(8,128)S(1)}, f32[256,1024]{1,0:T(8,128)S(1)}, u32[]{:S(2)}, u32[]{:S(2)}) %collective-permute-start.5) | collective-permute-done | bytes 1048608 | tf_op jit(solution)/shard_map/ppermute | solution.py:10
  217.4 0.4 fusion.33
  217.8 1.0 copy.6
  (18 shorter events, 0.2 us)
Async XLA Ops:
  6.5 210.9 %copy-start = (bf16[1,256,256]{2,1,0:T(8,128)(2,1)S(1)}, bf16[1,256,256]{2,1,0:T(8,128)(2,1)}, u32[]{:S(2)}) copy-start(bf16[1,256,256]{2,1,0:T(8,128)(2,1)} %param.9) | copy-start | bytes 393220
  6.5 34.2 %all-gather.13.cloned.1.call-start = ((), (), s32[]{:S(2)}) async-start(), calls=%async_computation | async-start | bytes 1966080 | tf_op jit(solution)/shard_map/all_gather | solution.py:18
  9.6 2.1 copy-start.2
  9.6 61.9 %all-gather.15.cloned.1.call-start = ((), (), s32[]{:S(2)}) async-start(), calls=%async_computation.1 | async-start | bytes 1966080 | tf_op jit(solution)/shard_map/all_gather | solution.py:18
  10.4 92.0 %all-gather.17.cloned.1.call-start = ((), (), s32[]{:S(2)}) async-start(), calls=%async_computation.2 | async-start | bytes 1966080 | tf_op jit(solution)/shard_map/all_gather | solution.py:18
  11.1 122.0 %all-gather.19.cloned.1.call-start = ((), (), s32[]{:S(2)}) async-start(), calls=%async_computation.3 | async-start | bytes 1966080 | tf_op jit(solution)/shard_map/all_gather | solution.py:18
  11.7 152.2 %all-gather.21.cloned.1.call-start = ((), (), s32[]{:S(2)}) async-start(), calls=%async_computation.4 | async-start | bytes 1966080 | tf_op jit(solution)/shard_map/all_gather | solution.py:18
  45.8 25.8 %collective-permute-start = (f32[256,1024]{1,0:T(8,128)S(1)}, f32[256,1024]{1,0:T(8,128)S(1)}, u32[]{:S(2)}, u32[]{:S(2)}) collective-permute-start(f32[256,1024]{1,0:T(8,128)S(1)} %fusion.12), channel_id=1, source_target_pairs={{252,0},{0,4},{4,8},{8,12},{12,16},{16,20},{20,24},{24,28},{28,32}... | collective-permute-start | bytes 3145736 | tf_op jit(solution)/shard_map/ppermute | solution.py:10
  45.9 148.7 %all-gather.23.cloned.1.call-start = ((), (), s32[]{:S(2)}) async-start(), calls=%async_computation.5 | async-start | bytes 1966080 | tf_op jit(solution)/shard_map/all_gather | solution.py:18
  76.6 30.9 %collective-permute-start.1 = (f32[256,1024]{1,0:T(8,128)S(1)}, f32[256,1024]{1,0:T(8,128)S(1)}, u32[]{:S(2)}, u32[]{:S(2)}) collective-permute-start(f32[256,1024]{1,0:T(8,128)S(1)} %fusion.30), channel_id=1, source_target_pairs={{252,0},{0,4},{4,8},{8,12},{12,16},{16,20},{20,24},{24,28},{28,32}... | collective-permute-start | bytes 3145736 | tf_op jit(solution)/shard_map/ppermute | solution.py:10
  107.6 30.5 %collective-permute-start.2 = (f32[256,1024]{1,0:T(8,128)S(1)}, f32[256,1024]{1,0:T(8,128)S(1)}, u32[]{:S(2)}, u32[]{:S(2)}) collective-permute-start(f32[256,1024]{1,0:T(8,128)S(1)} %add.16), channel_id=1, source_target_pairs={{252,0},{0,4},{4,8},{8,12},{12,16},{16,20},{20,24},{24,28},{28,32}... | collective-permute-start | bytes 3145736 | tf_op jit(solution)/shard_map/ppermute | solution.py:10
  138.4 30.5 %collective-permute-start.3 = (f32[256,1024]{1,0:T(8,128)S(1)}, f32[256,1024]{1,0:T(8,128)S(1)}, u32[]{:S(2)}, u32[]{:S(2)}) collective-permute-start(f32[256,1024]{1,0:T(8,128)S(1)} %add.17), channel_id=1, source_target_pairs={{252,0},{0,4},{4,8},{8,12},{12,16},{16,20},{20,24},{24,28},{28,32}... | collective-permute-start | bytes 3145736 | tf_op jit(solution)/shard_map/ppermute | solution.py:10
  169.1 30.6 %collective-permute-start.4 = (f32[256,1024]{1,0:T(8,128)S(1)}, f32[256,1024]{1,0:T(8,128)S(1)}, u32[]{:S(2)}, u32[]{:S(2)}) collective-permute-start(f32[256,1024]{1,0:T(8,128)S(1)} %add.18), channel_id=1, source_target_pairs={{252,0},{0,4},{4,8},{8,12},{12,16},{16,20},{20,24},{24,28},{28,32}... | collective-permute-start | bytes 3145736 | tf_op jit(solution)/shard_map/ppermute | solution.py:10
  199.6 17.8 %copy-start.1 = (bf16[256,1024]{1,0:T(8,128)(2,1)S(1)}, bf16[256,1024]{1,0:T(8,128)(2,1)}, u32[]{:S(2)}) copy-start(bf16[256,1024]{1,0:T(8,128)(2,1)} %param.5) | copy-start | bytes 1572868
  199.8 17.6 %collective-permute-start.5 = (f32[256,1024]{1,0:T(8,128)S(1)}, f32[256,1024]{1,0:T(8,128)S(1)}, u32[]{:S(2)}, u32[]{:S(2)}) collective-permute-start(f32[256,1024]{1,0:T(8,128)S(1)} %add.19), channel_id=1, source_target_pairs={{252,0},{0,4},{4,8},{8,12},{12,16},{16,20},{20,24},{24,28},{28,32}... | collective-permute-start | bytes 3145736 | tf_op jit(solution)/shard_map/ppermute | solution.py:10
Sparse Core Ops, SparseCore 0:
  9.7 30.9 all-gather.12
  42.5 29.0 all-gather.14
  73.4 29.0 all-gather.16
  104.1 29.0 all-gather.18
  134.8 29.0 all-gather.20
  165.5 29.0 all-gather.22
where the time goes:
time: 226 us
  waiting for transfers between devices  171 us (76%)
  matrix products  30.8 us (14%)
  between operations  17.3 us (8%)
  local copies, waits for them, and re-layouts  4.73 us (2%)
    all_gather x6, waiting for transfers between devices, per_device(): lax.all_gather(factor[0, offset], 'rhs', axis=0, tiled=True)  152 us
    dot_general x6, matrix products, per_device(): jnp.dot(lax.all_gather(factor[0, offset], 'rhs', axis=0, tiled=True), sol...  30.4 us
    ppermute x6, waiting for transfers between devices, from_behind(): return lax.ppermute(block, axis, route)  17.5 us
  transfers between devices with their start and end apart: 12, of which 7 were waited for; matrix products, arithmetic and copies ran while one was open for 14% of the time, Pallas kernels for 0%

commit v1 on v0

--- a/solution.py
+++ b/solution.py
@@ -15,7 +15,10 @@
     carried = jnp.zeros((rhs_block.shape[0], rhs_block.shape[1]), jnp.float32)
     for offset in reversed(range(hop_count)):
         product_term = jnp.dot(
-            lax.all_gather(factor[0, offset], "rhs", axis=0, tiled=True),
+            jnp.concatenate(
+                lax.all_to_all(jnp.stack([factor[0, offset]] * lax.psum(1, "rhs"), 0), "rhs", 0, 0),
+                0,
+            ),
             solution,
             preferred_element_type=jnp.float32,
         )

time: 226 us -> 176 us (0.78)
  waiting for transfers between devices: 171 us -> 71 us
  starting transfers between devices: 0.88 us -> 25.4 us
  blocking collectives: 0 us -> 24 us
  between operations: 17.3 us -> 3.9 us
  local copies, waits for them, and re-layouts: 4.73 us -> 13.6 us
  other arithmetic: 0.62 us -> 6.33 us
    all_gather x6 -> x0, waiting for transfers between devices: 152 us -> none  [per_device(): lax.all_gather(factor[0, offset], 'rhs', axis=0, tiled=True)]
    all_to_all x0 -> x5, waiting for transfers between devices: none -> 48.4 us  [per_device(): lax.all_to_all(jnp.stack([factor[0, offset]] * lax.psum(1, 'rhs'), 0), 'r...]
    all_to_all x0 -> x5, starting transfers between devices: none -> 25.1 us  [per_device(): lax.all_to_all(jnp.stack([factor[0, offset]] * lax.psum(1, 'rhs'), 0), 'r...]
    all_to_all x0 -> x1, blocking collectives: none -> 24 us  [per_device(): lax.all_to_all(jnp.stack([factor[0, offset]] * lax.psum(1, 'rhs'), 0), 'r...]
    another operation x0 -> x7, local copies, waits for them, and re-layouts: none -> 11.9 us  [per_device(): jnp.stack([factor[0, offset]] * lax.psum(1, 'rhs'), 0)]
    add x4, other arithmetic: 0.62 us -> 6.33 us  [per_device(): carried = carried + product_term * tile_list[0, offset].astype(jnp.float32)]
    ppermute x6, waiting for transfers between devices: 17.5 us -> 22.6 us  [from_behind(): return lax.ppermute(block, axis, route)]
    slice x1 -> x0, local copies, waits for them, and re-layouts: 3.04 us -> none  [per_device(): factor[0, offset]]
  transfers between devices with their start and end apart: 12 -> 11, of which waited for: 7 -> 7; matrix products, arithmetic and copies ran while one was open for 14% -> 25% of each run, Pallas kernels for 0% -> 0%
where the time goes in v1:
time: 176 us; the launch traced here: 175 us
  waiting for transfers between devices  71 us (40%)
  matrix products  30.6 us (17%)
  starting transfers between devices  25.4 us (14%)
  blocking collectives  24 us (14%)
  local copies, waits for them, and re-layouts  13.6 us (8%)
  other arithmetic  6.33 us (4%)
  between operations  3.9 us (2%)
    all_to_all x5, waiting for transfers between devices, per_device(): lax.all_to_all(jnp.stack([factor[0, offset]] * lax.psum(1, 'rhs'), 0), 'r...  48.4 us
    dot_general x6, matrix products, per_device(): jnp.dot(jnp.concatenate(lax.all_to_all(jnp.stack([factor[0, offset]] * la...  30.2 us
    all_to_all x5, starting transfers between devices, per_device(): lax.all_to_all(jnp.stack([factor[0, offset]] * lax.psum(1, 'rhs'), 0), 'r...  25.1 us
    all_to_all x1, blocking collectives, per_device(): lax.all_to_all(jnp.stack([factor[0, offset]] * lax.psum(1, 'rhs'), 0), 'r...  24 us
    ppermute x6, waiting for transfers between devices, from_behind(): return lax.ppermute(block, axis, route)  22.6 us
    another operation x7, local copies, waits for them, and re-layouts, per_device(): jnp.stack([factor[0, offset]] * lax.psum(1, 'rhs'), 0)  11.9 us
    add x4, other arithmetic, per_device(): carried = carried + product_term * tile_list[0, offset].astype(jnp.float32)  6.33 us
  transfers between devices with their start and end apart: 11, of which 7 were waited for; matrix products, arithmetic and copies ran while one was open for 25% of the time, Pallas kernels for 0%

profile of v1, /device:TPU:8, one launch (start us, length us, event | category | flops | bytes accessed | tf_op | source)
XLA Modules:
  0.0 174.8 jit_solution(14456160461273200498)
XLA Ops:
  0.0 2.8 %slice_bitcast_fusion = (bf16[64,3072]{1,0:T(8,128)(2,1)}, bf16[64,3072]{1,0:T(8,128)(2,1)}, bf16[64,3072]{1,0:T(8,128)(2,1)}, bf16[64,3072]{1,0:T(8,128)(2,1)S(...) fusion(bf16[1,6,64,3072]{3,2,1,0:T(8,128)(2,1)} %param.7), kind=kLoop, calls=%fused_computation.10 | loop fusion | bytes 4718592 | tf_op jit(solution)/shard_map/stack;squeeze | solution.py:19
  3.0 24.0 %all_to_all.30 = bf16[4,64,3072]{2,1,0:T(8,128)(2,1)S(1)} all-to-all(bf16[4,64,3072]{2,1,0:T(8,128)(2,1)S(1)} %stack.18), channel_id=1, replica_groups=mesh['col'=64,'rhs'=4] {'rhs'}, dimensions={0} | all-to-all | bytes 3145728 | tf_op jit(solution)/shard_map/all_to_all | solution.py:19
  26.9 1.3 stack.19
  28.3 5.1 %all-to-all-start.1 = ((bf16[4,64,3072]{2,1,0:T(8,128)(2,1)}), bf16[4,64,3072]{2,1,0:T(8,128)(2,1)S(1)}, u32[]{:S(2)}, u32[]{:S(2)}) async-start(bf16[4,64,3072]{2,1,0:T(8,128)(2,1)} %stack.19), calls=%async_computation.1 | async-start | bytes 3145728 | tf_op jit(solution)/shard_map/all_to_all | solution.py:19
  33.4 0.7 fusion.3
  34.7 5.6 %convolution_multiply_fusion.5 = f32[256,1024]{1,0:T(8,128)} fusion(bf16[256,3072]{1,0:T(8,128)(2,1)S(1)} %bitcast.46, bf16[3072,1024]{1,0:T(8,128)(2,1)} %param.6, f32[]{:T(128)} %bitcast.2), kind=kOutput, calls=%fused_computation.5 | convolution fusion | flops 1610874880 | bytes 8912900 | tf_op jit(solution)/shard_map/dot_general | solution.py:17
  40.3 11.5 %all-to-all-done.1 = bf16[4,64,3072]{2,1,0:T(8,128)(2,1)S(1)} async-done(((bf16[4,64,3072]{2,1,0:T(8,128)(2,1)}), bf16[4,64,3072]{2,1,0:T(8,128)(2,1)S(1)}, u32[]{:S(2)}, u32[]{:S(2)}) %all-to-all-start.1) | async-done | bytes 1572896 | tf_op jit(solution)/shard_map/all_to_all | solution.py:19
  51.8 2.3 %stack.20 = bf16[4,64,3072]{2,1,0:T(8,128)(2,1)} broadcast(bf16[64,3072]{1,0:T(8,128)(2,1)} %get-tuple-element.7), dimensions={1,2} | broadcast | bytes 1966080 | tf_op jit(solution)/shard_map/stack | solution.py:19
  54.1 5.0 %all-to-all-start.2 = ((bf16[4,64,3072]{2,1,0:T(8,128)(2,1)}), bf16[4,64,3072]{2,1,0:T(8,128)(2,1)S(1)}, u32[]{:S(2)}, u32[]{:S(2)}) async-start(bf16[4,64,3072]{2,1,0:T(8,128)(2,1)} %stack.20), calls=%async_computation.2 | async-start | bytes 3145728 | tf_op jit(solution)/shard_map/all_to_all | solution.py:19
  59.7 5.8 %fusion = f32[256,1024]{1,0:T(8,128)} fusion(f32[256,1024]{1,0:T(8,128)} %collective-permute-done, bf16[256,3072]{1,0:T(8,128)(2,1)S(1)} %bitcast.41, bf16[3072,1024]{1,0:T(8,128)(2,1)} %param.6, f32[]{:T(128)} %bitcast.5), kind=kOutput, calls=%fused_computation.6 | convolution fusion | flops 1611137024 | bytes 9961476 | tf_op jit(solution)/shard_map/dot_general | solution.py:17
  65.5 11.3 %all-to-all-done.2 = bf16[4,64,3072]{2,1,0:T(8,128)(2,1)S(1)} async-done(((bf16[4,64,3072]{2,1,0:T(8,128)(2,1)}), bf16[4,64,3072]{2,1,0:T(8,128)(2,1)S(1)}, u32[]{:S(2)}, u32[]{:S(2)}) %all-to-all-start.2) | async-done | bytes 1572896 | tf_op jit(solution)/shard_map/all_to_all | solution.py:19
  76.8 2.6 %stack.21 = bf16[4,64,3072]{2,1,0:T(8,128)(2,1)} broadcast(bf16[64,3072]{1,0:T(8,128)(2,1)} %get-tuple-element.6), dimensions={1,2} | broadcast | bytes 1966080 | tf_op jit(solution)/shard_map/stack | solution.py:19
  79.4 5.0 %all-to-all-start.3 = ((bf16[4,64,3072]{2,1,0:T(8,128)(2,1)}), bf16[4,64,3072]{2,1,0:T(8,128)(2,1)S(1)}, u32[]{:S(2)}, u32[]{:S(2)}) async-start(bf16[4,64,3072]{2,1,0:T(8,128)(2,1)} %stack.21), calls=%async_computation.3 | async-start | bytes 3145728 | tf_op jit(solution)/shard_map/all_to_all | solution.py:19
  85.0 5.1 %convolution_multiply_fusion.3 = f32[256,1024]{1,0:T(8,128)S(1)} fusion(bf16[256,3072]{1,0:T(8,128)(2,1)} %bitcast.44, bf16[3072,1024]{1,0:T(8,128)(2,1)} %param.6, f32[]{:T(128)} %bitcast.8), kind=kOutput, calls=%fused_computation.3 | convolution fusion | flops 1610874880 | bytes 8912900 | tf_op jit(solution)/shard_map/dot_general | solution.py:17
  90.1 1.1 add.16
  91.2 9.9 %all-to-all-done.3 = bf16[4,64,3072]{2,1,0:T(8,128)(2,1)S(1)} async-done(((bf16[4,64,3072]{2,1,0:T(8,128)(2,1)}), bf16[4,64,3072]{2,1,0:T(8,128)(2,1)S(1)}, u32[]{:S(2)}, u32[]{:S(2)}) %all-to-all-start.3) | async-done | bytes 1572896 | tf_op jit(solution)/shard_map/all_to_all | solution.py:19
  101.2 1.3 stack.22
  102.5 5.0 %all-to-all-start.4 = ((bf16[4,64,3072]{2,1,0:T(8,128)(2,1)}), bf16[4,64,3072]{2,1,0:T(8,128)(2,1)S(1)}, u32[]{:S(2)}, u32[]{:S(2)}) async-start(bf16[4,64,3072]{2,1,0:T(8,128)(2,1)} %stack.22), calls=%async_computation.4 | async-start | bytes 3145728 | tf_op jit(solution)/shard_map/all_to_all | solution.py:19
  108.1 4.6 %convolution_multiply_fusion.2 = f32[256,1024]{1,0:T(8,128)S(1)} fusion(bf16[256,3072]{1,0:T(8,128)(2,1)S(1)} %bitcast.43, bf16[3072,1024]{1,0:T(8,128)(2,1)} %param.6, f32[]{:T(128)} %bitcast.11), kind=kOutput, calls=%fused_computation.2 | convolution fusion | flops 1610874880 | bytes 8912900 | tf_op jit(solution)/shard_map/dot_general | solution.py:17
  112.7 2.4 %add.17 = f32[256,1024]{1,0:T(8,128)} add(f32[256,1024]{1,0:T(8,128)} %collective-permute-done.2, f32[256,1024]{1,0:T(8,128)S(1)} %convolution_multiply_fusion.2) | non-fusion elementwise | flops 262144 | bytes 3145728 | tf_op jit(solution)/shard_map/add | solution.py:25
  115.1 8.4 %all-to-all-done.4 = bf16[4,64,3072]{2,1,0:T(8,128)(2,1)S(1)} async-done(((bf16[4,64,3072]{2,1,0:T(8,128)(2,1)}), bf16[4,64,3072]{2,1,0:T(8,128)(2,1)S(1)}, u32[]{:S(2)}, u32[]{:S(2)}) %all-to-all-start.4) | async-done | bytes 1572896 | tf_op jit(solution)/shard_map/all_to_all | solution.py:19
  123.5 1.4 stack.23
  124.9 5.0 %all-to-all-start.5 = ((bf16[4,64,3072]{2,1,0:T(8,128)(2,1)}), bf16[4,64,3072]{2,1,0:T(8,128)(2,1)S(1)}, u32[]{:S(2)}, u32[]{:S(2)}) async-start(bf16[4,64,3072]{2,1,0:T(8,128)(2,1)} %stack.23), calls=%async_computation.5 | async-start | bytes 3145728 | tf_op jit(solution)/shard_map/all_to_all | solution.py:19
  130.5 4.6 %convolution_multiply_fusion.1 = f32[256,1024]{1,0:T(8,128)S(1)} fusion(bf16[256,3072]{1,0:T(8,128)(2,1)S(1)} %bitcast.42, bf16[3072,1024]{1,0:T(8,128)(2,1)} %param.6, f32[]{:T(128)} %bitcast.14), kind=kOutput, calls=%fused_computation.1 | convolution fusion | flops 1610874880 | bytes 8912900 | tf_op jit(solution)/shard_map/dot_general | solution.py:17
  135.1 1.4 add.18
  137.4 7.4 %all-to-all-done.5 = bf16[4,64,3072]{2,1,0:T(8,128)(2,1)S(1)} async-done(((bf16[4,64,3072]{2,1,0:T(8,128)(2,1)}), bf16[4,64,3072]{2,1,0:T(8,128)(2,1)S(1)}, u32[]{:S(2)}, u32[]{:S(2)}) %all-to-all-start.5) | async-done | bytes 1572896 | tf_op jit(solution)/shard_map/all_to_all | solution.py:19
  144.8 4.6 %convolution_multiply_fusion = f32[256,1024]{1,0:T(8,128)S(1)} fusion(bf16[256,3072]{1,0:T(8,128)(2,1)S(1)} %bitcast.45, bf16[3072,1024]{1,0:T(8,128)(2,1)} %param.6, f32[]{:T(128)} %bitcast.17), kind=kOutput, calls=%fused_computation | convolution fusion | flops 1610874880 | bytes 8912900 | tf_op jit(solution)/shard_map/dot_general | solution.py:17
  149.3 5.0 %collective-permute-done.4 = f32[256,1024]{1,0:T(8,128)} collective-permute-done((f32[256,1024]{1,0:T(8,128)S(1)}, f32[256,1024]{1,0:T(8,128)}, u32[]{:S(2)}, u32[]{:S(2)}) %collective-permute-start.4) | collective-permute-done | bytes 1048608 | tf_op jit(solution)/shard_map/ppermute | solution.py:10
  154.4 1.4 add.19
  155.8 17.5 %collective-permute-done.5 = f32[256,1024]{1,0:T(8,128)S(1)} collective-permute-done((f32[256,1024]{1,0:T(8,128)S(1)}, f32[256,1024]{1,0:T(8,128)S(1)}, u32[]{:S(2)}, u32[]{:S(2)}) %collective-permute-start.5) | collective-permute-done | bytes 1048608 | tf_op jit(solution)/shard_map/ppermute | solution.py:10
  173.4 0.4 fusion.1
  173.8 1.0 copy.6
  (23 shorter events, 0.6 us)
Async XLA Ops:
  0.0 173.4 %copy-start = (bf16[1,256,256]{2,1,0:T(8,128)(2,1)S(1)}, bf16[1,256,256]{2,1,0:T(8,128)(2,1)}, u32[]{:S(2)}) copy-start(bf16[1,256,256]{2,1,0:T(8,128)(2,1)} %param.9) | copy-start | bytes 393220
  28.3 5.1 %copy-start.5 = (s32[1,6]{1,0:T(1,128)S(1)}, s32[1,6]{1,0:T(1,128)}, u32[]{:S(2)}) copy-start(s32[1,6]{1,0:T(1,128)} %param.8) | copy-start | bytes 76
  28.3 23.5 %all-to-all-start.1 = ((bf16[4,64,3072]{2,1,0:T(8,128)(2,1)}), bf16[4,64,3072]{2,1,0:T(8,128)(2,1)S(1)}, u32[]{:S(2)}, u32[]{:S(2)}) async-start(bf16[4,64,3072]{2,1,0:T(8,128)(2,1)} %stack.19), calls=%async_computation.1 | async-start | bytes 3145728 | tf_op jit(solution)/shard_map/all_to_all | solution.py:19
  40.3 19.4 %collective-permute-start = (f32[256,1024]{1,0:T(8,128)}, f32[256,1024]{1,0:T(8,128)}, u32[]{:S(2)}, u32[]{:S(2)}) collective-permute-start(f32[256,1024]{1,0:T(8,128)} %convolution_multiply_fusion.5), channel_id=1, source_target_pairs={{252,0},{0,4},{4,8},{8,12},{12,16},{16,20},{20,24},{24,28},{28,32}... | collective-permute-start | bytes 3145736 | tf_op jit(solution)/shard_map/ppermute | solution.py:10
  54.1 22.6 %all-to-all-start.2 = ((bf16[4,64,3072]{2,1,0:T(8,128)(2,1)}), bf16[4,64,3072]{2,1,0:T(8,128)(2,1)S(1)}, u32[]{:S(2)}, u32[]{:S(2)}) async-start(bf16[4,64,3072]{2,1,0:T(8,128)(2,1)} %stack.20), calls=%async_computation.2 | async-start | bytes 3145728 | tf_op jit(solution)/shard_map/all_to_all | solution.py:19
  65.5 24.6 %collective-permute-start.1 = (f32[256,1024]{1,0:T(8,128)}, f32[256,1024]{1,0:T(8,128)S(1)}, u32[]{:S(2)}, u32[]{:S(2)}) collective-permute-start(f32[256,1024]{1,0:T(8,128)} %fusion), channel_id=1, source_target_pairs={{252,0},{0,4},{4,8},{8,12},{12,16},{16,20},{20,24},{24,28},{28,32}... | collective-permute-start | bytes 3145736 | tf_op jit(solution)/shard_map/ppermute | solution.py:10
  76.8 2.6 %copy-start.1 = (bf16[4,64,3072]{2,1,0:T(8,128)(2,1)}, bf16[4,64,3072]{2,1,0:T(8,128)(2,1)S(1)}, u32[]{:S(2)}) copy-start(bf16[4,64,3072]{2,1,0:T(8,128)(2,1)S(1)} %all-to-all-done.2) | copy-start | bytes 4718596
  79.4 21.8 %all-to-all-start.3 = ((bf16[4,64,3072]{2,1,0:T(8,128)(2,1)}), bf16[4,64,3072]{2,1,0:T(8,128)(2,1)S(1)}, u32[]{:S(2)}, u32[]{:S(2)}) async-start(bf16[4,64,3072]{2,1,0:T(8,128)(2,1)} %stack.21), calls=%async_computation.3 | async-start | bytes 3145728 | tf_op jit(solution)/shard_map/all_to_all | solution.py:19
  90.1 11.1 %copy-start.3 = (bf16[64,3072]{1,0:T(8,128)(2,1)S(1)}, bf16[64,3072]{1,0:T(8,128)(2,1)}, u32[]{:S(2)}) copy-start(bf16[64,3072]{1,0:T(8,128)(2,1)} %get-tuple-element.10) | copy-start | bytes 1179652
  91.2 21.5 %collective-permute-start.2 = (f32[256,1024]{1,0:T(8,128)}, f32[256,1024]{1,0:T(8,128)}, u32[]{:S(2)}, u32[]{:S(2)}) collective-permute-start(f32[256,1024]{1,0:T(8,128)} %add.16), channel_id=1, source_target_pairs={{252,0},{0,4},{4,8},{8,12},{12,16},{16,20},{20,24},{24,28},{28,32}... | collective-permute-start | bytes 3145736 | tf_op jit(solution)/shard_map/ppermute | solution.py:10
  102.5 21.0 %all-to-all-start.4 = ((bf16[4,64,3072]{2,1,0:T(8,128)(2,1)}), bf16[4,64,3072]{2,1,0:T(8,128)(2,1)S(1)}, u32[]{:S(2)}, u32[]{:S(2)}) async-start(bf16[4,64,3072]{2,1,0:T(8,128)(2,1)} %stack.22), calls=%async_computation.4 | async-start | bytes 3145728 | tf_op jit(solution)/shard_map/all_to_all | solution.py:19
  112.7 10.8 %copy-start.2 = (bf16[64,3072]{1,0:T(8,128)(2,1)S(1)}, bf16[64,3072]{1,0:T(8,128)(2,1)}, u32[]{:S(2)}) copy-start(bf16[64,3072]{1,0:T(8,128)(2,1)} %get-tuple-element.5) | copy-start | bytes 1179652
  115.1 19.9 %collective-permute-start.3 = (f32[256,1024]{1,0:T(8,128)}, f32[256,1024]{1,0:T(8,128)}, u32[]{:S(2)}, u32[]{:S(2)}) collective-permute-start(f32[256,1024]{1,0:T(8,128)} %add.17), channel_id=1, source_target_pairs={{252,0},{0,4},{4,8},{8,12},{12,16},{16,20},{20,24},{24,28},{28,32}... | collective-permute-start | bytes 3145736 | tf_op jit(solution)/shard_map/ppermute | solution.py:10
  124.9 19.9 %all-to-all-start.5 = ((bf16[4,64,3072]{2,1,0:T(8,128)(2,1)}), bf16[4,64,3072]{2,1,0:T(8,128)(2,1)S(1)}, u32[]{:S(2)}, u32[]{:S(2)}) async-start(bf16[4,64,3072]{2,1,0:T(8,128)(2,1)} %stack.23), calls=%async_computation.5 | async-start | bytes 3145728 | tf_op jit(solution)/shard_map/all_to_all | solution.py:19
  136.5 17.9 %collective-permute-start.4 = (f32[256,1024]{1,0:T(8,128)S(1)}, f32[256,1024]{1,0:T(8,128)}, u32[]{:S(2)}, u32[]{:S(2)}) collective-permute-start(f32[256,1024]{1,0:T(8,128)S(1)} %add.18), channel_id=1, source_target_pairs={{252,0},{0,4},{4,8},{8,12},{12,16},{16,20},{20,24},{24,28},{28,32}... | collective-permute-start | bytes 3145736 | tf_op jit(solution)/shard_map/ppermute | solution.py:10
  149.3 24.0 %copy-start.4 = (bf16[256,1024]{1,0:T(8,128)(2,1)S(1)}, bf16[256,1024]{1,0:T(8,128)(2,1)}, u32[]{:S(2)}) copy-start(bf16[256,1024]{1,0:T(8,128)(2,1)} %param.5) | copy-start | bytes 1572868
  155.8 17.6 %collective-permute-start.5 = (f32[256,1024]{1,0:T(8,128)S(1)}, f32[256,1024]{1,0:T(8,128)S(1)}, u32[]{:S(2)}, u32[]{:S(2)}) collective-permute-start(f32[256,1024]{1,0:T(8,128)S(1)} %add.19), channel_id=1, source_target_pairs={{252,0},{0,4},{4,8},{8,12},{12,16},{16,20},{20,24},{24,28},{28,32}... | collective-permute-start | bytes 3145736 | tf_op jit(solution)/shard_map/ppermute | solution.py:10
